TPU v7x, 32 devices: a whole 2x2x4 slice. The times are simulated.
32 devices in a mesh: row: 4 (over y, core), col: 8 (over z, x).
Axes of the slice: x: 2, y: 2, z: 4, core: 2. Of those that a mesh axis runs over, the one named last changes fastest.
Arguments:
- inverse: float32 [16384, 16384], P('row', 'col'), may hold values from -6 to 6
- front_blocks: int32 [2, 16], replicated, may hold values from 0 to 63, as said below
- panels: float32 [2, 4096, 256], P(None, 'row'), may hold values from -0.09375 to 0.09375
- diag_terms: float32 [2, 256, 256], replicated, may hold values from -6 to 6
- bounds: int32 [2, 4], replicated, may hold values from 1 to 128, 256 in all within a row
Outputs:
- border: float32 [2, 4096, 256], P(None, ('row', 'col'))
- diag_block: float32 [2, 256, 256], replicated
Inputs may be any that keep to these rules, and one draw needn't show every extreme that they name: `front_blocks`: each row names 16 distinct blocks. Positions 4 r to 4 r + 3 name blocks of four different groups of 16 consecutive blocks, and every such group is named at exactly four positions, of four different r. Positions 2 o and 2 o + 1 name blocks of two different groups of 8 consecutive blocks, and every such group is named at exactly two positions, of two different o.
All inputs are finite; a program needn't handle non-finite values.
Results may differ from a plain program's by a relative error of at most 0.0001.
Values sent between devices are 32-bit elements; how exact they have to be, the bound alone decides.
A program may use at most 128 MiB of HBM per device.

v0:
```python
import jax
import jax.numpy as jnp
from jax import lax
from jax.sharding import PartitionSpec as P

BS = 256


def body(inverse, front_blocks, panels, diag_terms, bounds):
    n_row = lax.axis_size("row")
    n_col = lax.axis_size("col")
    row_index = lax.axis_index("row")
    col_index = lax.axis_index("col")
    rows_loc, cols_loc = inverse.shape
    row_group = rows_loc // BS
    col_group = cols_loc // BS
    list_length = front_blocks.shape[1]
    per_owner = list_length // n_row
    highest = lax.Precision.HIGHEST
    borders = []
    diagonals = []
    for front_index in range(2):
        front_list = front_blocks[front_index]
        own_blocks = lax.dynamic_slice_in_dim(front_list, row_index * per_owner, per_owner)
        w_loc = panels[front_index]
        panel_width = w_loc.shape[1]
        w_pieces = w_loc.reshape(per_owner, BS, panel_width)
        targets = col_index * col_group + jnp.arange(col_group, dtype=jnp.int32)
        picker = (own_blocks[None, :] == targets[:, None]).astype(jnp.float32)
        own_piece = jnp.einsum("ki,iab->ab", picker, w_pieces, precision=highest)
        slot_rows = lax.all_gather(own_piece, "row", axis=0, tiled=True).reshape(
            n_row, BS, panel_width
        )
        owners = front_list.reshape(n_row, per_owner)
        placer = jnp.sum((owners[None, :, :] == targets[:, None, None]).astype(jnp.float32), axis=2)
        w_tilde = jnp.einsum("ks,sab->kab", placer, slot_rows, precision=highest).reshape(
            cols_loc, panel_width
        )
        dest_lists = front_list.reshape(n_row, per_owner)
        local_ids = row_index * row_group + jnp.arange(row_group, dtype=jnp.int32)
        share_rows = per_owner * BS // n_col
        full_rows = jnp.dot(inverse, w_tilde, precision=highest)
        quarters = BS // share_rows
        full_pieces = full_rows.reshape(row_group, quarters, share_rows, panel_width)
        first_rows = jnp.arange(n_col, dtype=jnp.int32) * share_rows
        dest_block = dest_lists[:, first_rows // BS]
        block_pick = (dest_block.T[:, :, None] == local_ids[None, None, :]).astype(jnp.float32)
        quarter_pick = (
            (first_rows % BS // share_rows)[:, None]
            == jnp.arange(quarters, dtype=jnp.int32)[None, :]
        ).astype(jnp.float32)
        sectioned = jnp.einsum("cq,kqap->ckap", quarter_pick, full_pieces, precision=highest)
        ordered = jnp.einsum("cdk,ckap->cdap", block_pick, sectioned, precision=highest)
        ordered = ordered.reshape(n_col * n_row * share_rows, panel_width)
        reduced = lax.psum_scatter(ordered, "col", scatter_dimension=0, tiled=True)
        received = lax.all_to_all(
            reduced.reshape(n_row, share_rows, panel_width),
            "row",
            split_axis=0,
            concat_axis=0,
            tiled=True,
        )
        product = jnp.sum(received, axis=0)
        w_mine = lax.dynamic_slice_in_dim(w_loc, col_index * share_rows, share_rows, 0)
        own_term = jnp.dot(w_mine.T, product, precision=highest)
        summed_total = lax.psum(own_term, ("row", "col"))
        node_ends = jnp.cumsum(bounds[front_index])
        columns = jnp.arange(panel_width, dtype=jnp.int32)
        node_ids = jnp.sum((columns[:, None] >= node_ends[None, :]).astype(jnp.int32), axis=1)
        same_node = (node_ids[:, None] == node_ids[None, :]).astype(jnp.float32)
        borders.append(-product)
        diagonals.append(same_node * (diag_terms[front_index] + summed_total))
    return (jnp.stack(borders), jnp.stack(diagonals))


def solution(mesh):
    placed = (P("row", "col"), P(), P(None, "row", None), P(), P())
    return jax.shard_map(
        body,
        mesh=mesh,
        in_specs=placed,
        out_specs=(P(None, ("row", "col"), None), P()),
        check_vma=False,
    )
```

profile of v0, /device:TPU:0, one launch (start us, length us, event | category | flops | bytes accessed | tf_op | source)
XLA Modules:
  0.0 494.8 jit_solution(6554460476007873666)
XLA Ops:
  8.0 1.7 fusion.46
  10.0 2.3 fusion.6
  13.1 2.3 fusion.4
  17.2 15.4 %all-gather.3.cloned.1.call-done = f32[1024,256]{1,0:T(8,128)} async-done(((f32[256,256]{1,0:T(8,128)}), f32[1024,256]{1,0:T(8,128)}) %all-gather.3.cloned.1.call-update) | async-done | bytes 1048592 | tf_op jit(solution)/shard_map/all_gather | solution.py:31
  32.6 4.0 fusion.10
  37.4 69.0 %convolution_bitcast_fusion.1 = f32[4096,256]{0,1:T(8,128)} fusion(f32[2048,256]{1,0:T(8,128)S(1)} %bitcast.104, f32[4096,2048]{1,0:T(8,128)} %param.5), kind=kOutput, calls=%fused_computation.7 | convolution fusion | flops 25769803776 | bytes 39845888 | tf_op jit(solution)/shard_map/dot_general | solution.py:42
  106.3 6.6 %reshape.215 = f32[16,2,128,256]{2,1,0,3:T(2,128)} reshape(f32[4096,256]{0,1:T(8,128)} %convolution_bitcast_fusion.1) | data formatting | bytes 8388608 | tf_op jit(solution)/shard_map/reshape | solution.py:44
  112.9 9.3 %copy.20 = f32[16,2,128,256]{3,1,2,0:T(2,128)} copy(f32[16,2,128,256]{2,1,0,3:T(2,128)} %reshape.215) | data formatting | bytes 8388608 | tf_op jit(solution)/shard_map/reshape | solution.py:44
  122.2 11.7 %fusion.34 = f32[8,16,128,256]{3,0,2,1:T(8,128)S(1)} fusion(f32[16,2,128,256]{3,1,2,0:T(2,128)} %copy.20, s32[8]{0:T(128)S(1)} %and_select_fusion), kind=kOutput, calls=%fused_computation.58 | convolution fusion | flops 100663312 | bytes 20971552 | tf_op jit(solution)/shard_map/cq,kqap->ckap/dot_general | solution.py:52
  133.9 12.2 %fusion.2 = f32[8,4,128,256]{3,1,2,0:T(4,128)S(1)} fusion(f32[8,16,128,256]{3,0,2,1:T(8,128)S(1)} %fusion.34, s32[16]{0:T(128)S(1)} %iota_add_fusion.1, s32[8,4]{1,0:T(8,128)S(1)} %gather_fusion), kind=kOutput, calls=%fused_computation.4 | convolution fusion | flops 201327104 | bytes 20971712 | tf_op jit(solution)/shard_map/cdk,ckap->cdap/dot_general | solution.py:53
  146.1 2.7 copy.22
  149.5 4.0 fusion.8
  154.2 58.9 %convolution_bitcast_fusion = f32[4096,256]{0,1:T(8,128)} fusion(f32[2048,256]{1,0:T(8,128)S(1)} %bitcast.105, f32[4096,2048]{1,0:T(8,128)} %param.5), kind=kOutput, calls=%fused_computation.6 | convolution fusion | flops 25769803776 | bytes 39845888 | tf_op jit(solution)/shard_map/dot_general | solution.py:42
  213.2 6.6 %reshape.220 = f32[16,2,128,256]{2,1,0,3:T(2,128)} reshape(f32[4096,256]{0,1:T(8,128)} %convolution_bitcast_fusion) | data formatting | bytes 8388608 | tf_op jit(solution)/shard_map/reshape | solution.py:44
  219.8 9.3 %copy.26 = f32[16,2,128,256]{3,1,2,0:T(2,128)} copy(f32[16,2,128,256]{2,1,0,3:T(2,128)} %reshape.220) | data formatting | bytes 8388608 | tf_op jit(solution)/shard_map/reshape | solution.py:44
  229.2 11.7 %fusion.32 = f32[8,16,128,256]{3,0,2,1:T(8,128)S(1)} fusion(f32[16,2,128,256]{3,1,2,0:T(2,128)} %copy.26, s32[8]{0:T(128)S(1)} %and_select_fusion), kind=kOutput, calls=%fused_computation.56 | convolution fusion | flops 100663312 | bytes 20971552 | tf_op jit(solution)/shard_map/cq,kqap->ckap/dot_general | solution.py:52
  240.9 12.2 %fusion = f32[8,4,128,256]{3,1,2,0:T(4,128)S(1)} fusion(f32[8,16,128,256]{3,0,2,1:T(8,128)S(1)} %fusion.32, s32[8,4]{1,0:T(8,128)S(1)} %gather_fusion.1, s32[16]{0:T(128)S(1)} %iota_add_fusion.1), kind=kOutput, calls=%fused_computation.2 | convolution fusion | flops 201327104 | bytes 20971712 | tf_op jit(solution)/shard_map/cdk,ckap->cdap/dot_general | solution.py:53
  253.1 2.7 copy.28
  255.9 3.6 all-to-all-start
  260.0 84.4 %reduce-scatter.5.cloned.1.call-done = f32[512,256]{1,0:T(8,128)} async-done(((f32[4096,256]{1,0:T(8,128)}), f32[512,256]{1,0:T(8,128)}) %reduce-scatter.5.cloned.1.call-update) | async-done | bytes 524304 | tf_op jit(solution)/shard_map/reduce_scatter | solution.py:55
  344.4 3.5 all-to-all-start.1
  347.9 2.1 fusion.18
  350.0 6.6 %all-to-all-done.1 = f32[4,128,256]{2,1,0:T(8,128)S(1)} async-done(((f32[4,128,256]{2,1,0:T(8,128)}), f32[4,128,256]{2,1,0:T(8,128)S(1)}, u32[]{:S(2)}, u32[]{:S(2)}) %all-to-all-start.1) | async-done | bytes 524320 | tf_op jit(solution)/shard_map/all_to_all | solution.py:56
  358.5 127.5 %all-reduce.3.cloned.1.call-done = (f32[256,256]{1,0:T(8,128)}, f32[256,256]{1,0:T(8,128)}) async-done(((f32[256,256]{1,0:T(8,128)}, f32[256,256]{1,0:T(8,128)}), (f32[256,256]{1,0:T(8,128)}, f32[256,256]{1,0:T(8,128)})) %all-reduce.3.cloned.1.call-update) | async-done | bytes 524304 | tf_op jit(solution)/shard_map/psum | solution.py:66
  (50 shorter events, 10.2 us)
Async XLA Ops:
  7.2 25.5 %all-gather.3.cloned.1.call-start = ((), (), s32[]{:S(2)}) async-start(), calls=%async_computation.4 | async-start | bytes 1310720 | tf_op jit(solution)/shard_map/all_gather | solution.py:31
  9.7 27.7 %copy-start = (f32[1,1024,256]{2,1,0:T(8,128)}, f32[1,1024,256]{2,1,0:T(8,128)S(1)}, u32[]{:S(2)}) copy-start(f32[1,1024,256]{2,1,0:T(8,128)S(1)} %get-tuple-element.10) | copy-start | bytes 3145732
  13.1 136.5 %all-gather.5.cloned.1.call-start = ((), (), s32[]{:S(2)}) async-start(), calls=%async_computation.6 | async-start | bytes 1310720 | tf_op jit(solution)/shard_map/all_gather | solution.py:31
  16.2 239.7 %reduce-scatter.3.cloned.1.call-start = ((), (), s32[]{:S(2)}) async-start(), calls=%async_computation.5 | async-start | bytes 4718592 | tf_op jit(solution)/shard_map/reduce_scatter | solution.py:55
  148.8 195.5 %reduce-scatter.5.cloned.1.call-start = ((), (), s32[]{:S(2)}) async-start(), calls=%async_computation.7 | async-start | bytes 4718592 | tf_op jit(solution)/shard_map/reduce_scatter | solution.py:55
  255.8 3.7 copy-start.2
  255.8 230.3 %copy-start.1 = (f32[2,256,256]{2,1,0:T(8,128)S(1)}, f32[2,256,256]{2,1,0:T(8,128)}, u32[]{:S(2)}) copy-start(f32[2,256,256]{2,1,0:T(8,128)} %param.8) | copy-start | bytes 1572868
  255.9 88.5 %all-to-all-start = ((f32[4,128,256]{2,1,0:T(8,128)}), f32[4,128,256]{2,1,0:T(8,128)S(1)}, u32[]{:S(2)}, u32[]{:S(2)}) async-start(f32[4,128,256]{2,1,0:T(8,128)} %bitcast.112), calls=%async_computation.1 | async-start | bytes 1048576 | tf_op jit(solution)/shard_map/all_to_all | solution.py:56
  344.4 12.3 %all-to-all-start.1 = ((f32[4,128,256]{2,1,0:T(8,128)}), f32[4,128,256]{2,1,0:T(8,128)S(1)}, u32[]{:S(2)}, u32[]{:S(2)}) async-start(f32[4,128,256]{2,1,0:T(8,128)} %bitcast.113), calls=%async_computation.3 | async-start | bytes 1048576 | tf_op jit(solution)/shard_map/all_to_all | solution.py:56
  347.8 138.2 %all-reduce.3.cloned.1.call-start = ((), (), s32[]{:S(2)}) async-start(), calls=%async_computation.8 | async-start | bytes 1048576 | tf_op jit(solution)/shard_map/psum | solution.py:66
Sparse Core Ops, SparseCore 0:
  13.2 19.4 all-gather.2
  34.8 16.6 all-gather.4
  148.9 88.2 reduce-scatter.2
  256.0 88.3 reduce-scatter.4
  357.9 128.1 all-reduce.2
where the time goes:
time: 497 us; the launch traced here: 495 us
  waiting for transfers between devices  234 us (47%)
  matrix products  192 us (39%)
  local copies, waits for them, and re-layouts  44 us (9%)
  between operations  14.2 us (3%)
  starting transfers between devices  7.29 us (1%)
    dot_general x2, matrix products, body(): full_rows = jnp.dot(inverse, w_tilde, precision=highest)  128 us
    psum x1, waiting for transfers between devices, body(): summed_total = lax.psum(own_term, ('row', 'col'))  128 us
    reduce_scatter x2, waiting for transfers between devices, body(): reduced = lax.psum_scatter(ordered, 'col', scatter_dimension=0, tiled=True)  84.4 us
    reshape x4, local copies, waits for them, and re-layouts, body(): full_rows.reshape(row_group, quarters, share_rows, panel_width)  31.9 us
    dot_general x2, matrix products, body(): jnp.einsum('cdk,ckap->cdap', block_pick, sectioned, precision=highest)  24.4 us
    dot_general x2, matrix products, body(): jnp.einsum('cq,kqap->ckap', quarter_pick, full_pieces, precision=highest)  23.4 us
    all_gather x2, waiting for transfers between devices, body(): lax.all_gather(own_piece, 'row', axis=0, tiled=True)  15.4 us
  transfers between devices with their start and end apart: 7, of which 4 were waited for; matrix products, arithmetic and copies ran while one was open for 47% of the time, Pallas kernels for 0%

commit v1 on v0

v1 whole, which is shorter than its diff:
```python
import functools

import jax
import jax.numpy as jnp
from jax import lax
from jax.experimental import pallas as pl
from jax.experimental.pallas import tpu as pltpu
from jax.sharding import PartitionSpec as P

BS = 256


def split(a):
    hi = a.astype(jnp.bfloat16)
    lo = (a - hi.astype(jnp.float32)).astype(jnp.bfloat16)
    return hi, lo


def dot3(a, b):
    ah, al = a
    bh, bl = b
    dot = functools.partial(jnp.dot, preferred_element_type=jnp.float32)
    return dot(ah, bh) + (dot(ah, bl) + dot(al, bh))


def tile_kernel(dims, fb, inv, w, out, tiles, sem):
    fronts, kb, nr, nc, rg, cg, nz, nx = dims
    r = lax.axis_index("row")
    c = lax.axis_index("col")
    per_owner = kb // lax.axis_size("row")
    owners = []
    for f in range(fronts):
        rows = [jnp.int32(0)] * nr
        cols = [jnp.int32(0)] * nc
        own = [jnp.int32(0)] * nc
        n = jnp.int32(0)
        m = jnp.int32(0)
        for p in range(kb):
            b = fb[f, p]
            here = (b // rg) == r
            for i in range(nr):
                rows[i] = jnp.where(here & (n == i), b % rg, rows[i])
            n = n + here.astype(jnp.int32)
            there = (b // cg) == c
            for i in range(nc):
                hit = there & (m == i)
                cols[i] = jnp.where(hit, b % cg, cols[i])
                own[i] = jnp.where(hit, p // per_owner, own[i])
            m = m + there.astype(jnp.int32)
        owners.append(own)
        for k in range(nc):
            for i in range(nr):
                pltpu.make_async_copy(
                    inv.at[
                        pl.ds(pl.multiple_of(rows[i] * BS, BS), BS),
                        pl.ds(pl.multiple_of(cols[k] * BS, BS), BS),
                    ],
                    tiles.at[f, k, pl.ds(i * BS, BS)],
                    sem.at[f, k, i],
                ).start()
    sub = BS // (nz * nx)
    for f in range(fronts):
        total = None
        for k in range(nc):
            for i in range(nr):
                pltpu.make_async_copy(
                    inv.at[pl.ds(0, BS), pl.ds(0, BS)],
                    tiles.at[f, k, pl.ds(i * BS, BS)],
                    sem.at[f, k, i],
                ).wait()
            term = dot3(split(tiles[f, k]), split(w[owners[f][k], f]))
            total = term if total is None else total + term
        for i in range(nr):
            for s in range(nx):
                for z in range(nz):
                    at = i * BS + (s * nz + z) * sub
                    out[z * nx + s, f, i] = total[at : at + sub]


def body(inverse, front_blocks, panels, diag_terms, bounds):
    n_row = lax.axis_size("row")
    n_col = lax.axis_size("col")
    r = lax.axis_index("row")
    c = lax.axis_index("col")
    rows_loc, cols_loc = inverse.shape
    rg = rows_loc // BS
    cg = cols_loc // BS
    fronts, kb = front_blocks.shape
    width = panels.shape[2]
    per_owner = kb // n_row
    nr = kb // n_row
    nc = kb // n_col
    nz = per_owner
    nx = n_col // nz
    sub = BS // n_col
    share = nz * sub

    owner_rows = front_blocks.reshape(fronts, n_row, per_owner)
    mine = lax.dynamic_index_in_dim(owner_rows, r, 1, keepdims=False)
    pick = (mine // cg) == c
    pieces = panels.reshape(fronts, per_owner, BS, width)
    own_piece = jnp.sum(jnp.where(pick[:, :, None, None], pieces, 0.0), axis=1)
    gathered = lax.all_gather(own_piece, "row", axis=0, tiled=False)

    dims = (fronts, kb, nr, nc, rg, cg, nz, nx)
    partial = pl.pallas_call(
        functools.partial(tile_kernel, dims),
        out_shape=jax.ShapeDtypeStruct((n_col, fronts, nr, sub, width), jnp.float32),
        in_specs=[
            pl.BlockSpec(memory_space=pltpu.SMEM),
            pl.BlockSpec(memory_space=pl.ANY),
            pl.BlockSpec(memory_space=pltpu.VMEM),
        ],
        out_specs=pl.BlockSpec(memory_space=pltpu.VMEM),
        scratch_shapes=[
            pltpu.VMEM((fronts, nc, nr * BS, BS), jnp.float32),
            pltpu.SemaphoreType.DMA((fronts, nc, nr)),
        ],
        compiler_params=pltpu.CompilerParams(vmem_limit_bytes=40 << 20),
    )(front_blocks, inverse, gathered)

    reduced = lax.psum_scatter(partial, "col", scatter_dimension=0, tiled=False)
    groups = front_blocks // rg
    if nr == n_row:
        slots = jnp.swapaxes(reduced, 0, 1)
    else:
        named = jnp.any((groups == r).reshape(fronts, n_row, per_owner), axis=-1)
        place = jnp.cumsum(named.astype(jnp.int32), axis=1) - 1
        chosen = named[:, :, None] & (place[:, :, None] == jnp.arange(nr))
        slots = jnp.sum(
            jnp.where(chosen.transpose(1, 0, 2)[..., None, None], reduced[None], 0.0), axis=2
        )
    received = lax.all_to_all(slots, "row", split_axis=0, concat_axis=0, tiled=True)
    sources = lax.dynamic_index_in_dim(
        groups.reshape(fronts, n_row, per_owner), r, 1, keepdims=False
    )
    chosen = sources.T[:, None, :] == jnp.arange(n_row, dtype=jnp.int32)[None, :, None]
    ordered = jnp.sum(jnp.where(chosen[..., None, None], received[None], 0.0), axis=1)
    lines = [[z * nx + s for z in range(nz)] for s in range(nx)]
    product = lax.all_to_all(
        ordered, "col", split_axis=0, concat_axis=0, axis_index_groups=lines, tiled=True
    )
    product = jnp.swapaxes(product, 0, 1).reshape(fronts, share, width)
    w_mine = lax.dynamic_slice_in_dim(panels, c * share, share, 1)
    own_term = jnp.einsum(
        "fsa,fsb->fab", w_mine, product, precision=lax.Precision.HIGHEST
    )
    summed = lax.psum(own_term, ("row", "col"))
    ends = jnp.cumsum(bounds, axis=1)
    columns = jnp.arange(width, dtype=jnp.int32)
    ids = jnp.sum((columns[None, :, None] >= ends[:, None, :]).astype(jnp.int32), axis=2)
    same = (ids[:, :, None] == ids[:, None, :]).astype(jnp.float32)
    return (-product, same * (diag_terms + summed))


def solution(mesh):
    placed = (P("row", "col"), P(), P(None, "row", None), P(), P())
    return jax.shard_map(
        body,
        mesh=mesh,
        in_specs=placed,
        out_specs=(P(None, ("row", "col"), None), P()),
        check_vma=False,
    )
```

time: 497 us -> 277 us (0.56)
  matrix products: 192 us -> 2.38 us
  local copies, waits for them, and re-layouts: 44 us -> 4.24 us
  Pallas kernels: 0 us -> 7.14 us
    dot_general x12 -> x1, matrix products: 192 us -> 2.38 us  [body(): jnp.einsum('fsa,fsb->fab', w_mine, product, precision=lax.Precision.HIGHEST)]
    reshape x4 -> x2, local copies, waits for them, and re-layouts: 31.9 us -> 0.84 us  [the longest x1 0.76 us: body(): owner_rows = front_blocks.reshape(fronts, n_row, per_owner)]
    reduce_scatter x2 -> x1, waiting for transfers between devices: 84.4 us -> 68.5 us  [body(): reduced = lax.psum_scatter(partial, 'col', scatter_dimension=0, tiled=False)]
    all_gather x2 -> x1, waiting for transfers between devices: 15.4 us -> 25.4 us  [body(): gathered = lax.all_gather(own_piece, 'row', axis=0, tiled=False)]
    dot_general x6 -> x0, local copies, waits for them, and re-layouts: 8.18 us -> none  [the longest x2 5.38 us: body(): jnp.einsum('cdk,ckap->cdap', block_pick, sectioned, precision=highest)]
    all_to_all x2, waiting for transfers between devices: 6.62 us -> 14.6 us  [the longest x1 8.62 us: body(): lax.all_to_all(ordered, 'col', split_axis=0, concat_axis=0, axis_index_gr...]
    pallas_call x0 -> x1, Pallas kernels: none -> 7.14 us  [body(): pl.pallas_call(functools.partial(tile_kernel, dims), out_shape=jax.ShapeD...]
  transfers between devices with their start and end apart: 7 -> 5, of which waited for: 4 -> 5; matrix products, arithmetic and copies ran while one was open for 47% -> 0% of each run, Pallas kernels for 0% -> 0%
where the time goes in v1:
time: 277 us; the launch traced here: 276 us
  waiting for transfers between devices  234 us (84%)
  between operations  13.8 us (5%)
  other arithmetic  7.18 us (3%)
  Pallas kernels  7.14 us (3%)
  starting transfers between devices  7.07 us (3%)
  local copies, waits for them, and re-layouts  4.24 us (2%)
    psum x1, waiting for transfers between devices, body(): summed = lax.psum(own_term, ('row', 'col'))  126 us
    reduce_scatter x1, waiting for transfers between devices, body(): reduced = lax.psum_scatter(partial, 'col', scatter_dimension=0, tiled=False)  68.5 us
    all_gather x1, waiting for transfers between devices, body(): gathered = lax.all_gather(own_piece, 'row', axis=0, tiled=False)  25.4 us
    all_to_all x1, waiting for transfers between devices, body(): lax.all_to_all(ordered, 'col', split_axis=0, concat_axis=0, axis_index_gr...  8.62 us
    pallas_call x1, Pallas kernels, body(): pl.pallas_call(functools.partial(tile_kernel, dims), out_shape=jax.ShapeD...  7.14 us
    all_to_all x1, waiting for transfers between devices, body(): lax.all_to_all(slots, 'row', split_axis=0, concat_axis=0, tiled=True)  5.96 us
  transfers between devices with their start and end apart: 5, of which 5 were waited for; matrix products, arithmetic and copies ran while one was open for 0% of the time, Pallas kernels for 0%

profile of v1, /device:TPU:0, one launch (start us, length us, event | category | flops | bytes accessed | tf_op | source)
XLA Modules:
  0.0 276.3 jit_solution(12422776301363555291)
XLA Ops:
  7.2 0.0 all-gather.3.cloned.1.call-start
  7.2 0.7 and_select_fusion.1
  7.9 0.8 reshape.57
  8.7 0.1 reshape.56
  8.8 2.7 select_reduce_fusion
  11.5 0.0 reduce-scatter.2.cloned.1.call-start
  11.5 25.4 %all-gather.3.cloned.1.call-done = f32[8,256,256]{2,1,0:T(8,128)} async-done(((f32[2,256,256]{2,1,0:T(8,128)}), f32[8,256,256]{2,1,0:T(8,128)}) %all-gather.3.cloned.1.call-update) | async-done | bytes 2097168 | tf_op jit(solution)/shard_map/all_gather | solution.py:103
  36.9 1.6 copy-done
  38.5 7.1 %shard_map.68 = f32[8,2,4,32,256]{4,3,2,1,0:T(8,128)} custom-call(s32[2,16]{1,0:T(2,128)S(1)} %copy-done.1, f32[4096,2048]{1,0:T(8,128)} %inv.1, f32[4,2,256,256]{3,2,1,0:T(8,128)S(1)} %bitcast.13), custom_call_target="tpu_custom_call" | custom-call | tf_op jit(solution)/shard_map/pallas_call | solution.py:106
  45.7 0.1 copy.14
  45.8 68.5 %reduce-scatter.2.cloned.1.call-done = f32[1,2,4,32,256]{4,3,2,1,0:T(8,128)} async-done(((f32[8,2,4,32,256]{4,3,2,1,0:T(8,128)}), f32[1,2,4,32,256]{4,3,2,1,0:T(8,128)}) %reduce-scatter.2.cloned.1.call-update) | async-done | bytes 262160 | tf_op jit(solution)/shard_map/reduce_scatter | solution.py:122
  114.3 1.7 copy.15
  115.9 3.5 %all-to-all-start = ((f32[4,2,32,256]{3,2,1,0:T(8,128)}), f32[4,2,32,256]{3,2,1,0:T(8,128)S(1)}, u32[]{:S(2)}, u32[]{:S(2)}) async-start(f32[4,2,32,256]{3,2,1,0:T(8,128)} %copy.15), calls=%async_computation.1 | async-start | bytes 524288 | tf_op jit(solution)/shard_map/all_to_all | solution.py:133
  119.5 6.0 %all-to-all-done = f32[4,2,32,256]{3,2,1,0:T(8,128)S(1)} async-done(((f32[4,2,32,256]{3,2,1,0:T(8,128)}), f32[4,2,32,256]{3,2,1,0:T(8,128)S(1)}, u32[]{:S(2)}, u32[]{:S(2)}) %all-to-all-start) | async-done | bytes 262176 | tf_op jit(solution)/shard_map/all_to_all | solution.py:133
  125.5 0.8 select_reduce_fusion.1
  126.3 3.4 %all-to-all-start.1 = ((f32[4,2,32,256]{3,2,1,0:T(8,128)}), f32[4,2,32,256]{3,2,1,0:T(8,128)S(1)}, u32[]{:S(2)}, u32[]{:S(2)}) async-start(f32[4,2,32,256]{3,2,1,0:T(8,128)} %select_reduce_fusion.1), calls=%async_computation.2 | async-start | bytes 524288 | tf_op jit(solution)/shard_map/all_to_all | solution.py:140
  129.7 0.0 all-reduce.2.cloned.1.call-start
  129.8 0.2 reduce_window_sum.11
  130.0 8.6 %all-to-all-done.1 = f32[4,2,32,256]{3,2,1,0:T(8,128)S(1)} async-done(((f32[4,2,32,256]{3,2,1,0:T(8,128)}), f32[4,2,32,256]{3,2,1,0:T(8,128)S(1)}, u32[]{:S(2)}, u32[]{:S(2)}) %all-to-all-start.1) | async-done | bytes 262176 | tf_op jit(solution)/shard_map/all_to_all | solution.py:140
  138.6 2.4 fusion
  141.0 0.1 convert_reduce_fusion
  141.1 0.7 bitcast_negate_fusion
  141.8 126.0 %all-reduce.2.cloned.1.call-done = f32[2,256,256]{2,1,0:T(8,128)} async-done(((f32[2,256,256]{2,1,0:T(8,128)}), f32[2,256,256]{2,1,0:T(8,128)}) %all-reduce.2.cloned.1.call-update) | async-done | bytes 524304 | tf_op jit(solution)/shard_map/psum | solution.py:148
  267.8 2.0 add_select_fusion
  (14 shorter events, 0.1 us)
Async XLA Ops:
  7.2 29.8 %copy-start.1 = (s32[2,16]{1,0:T(2,128)S(1)}, s32[2,16]{1,0:T(2,128)}, u32[]{:S(2)}) copy-start(s32[2,16]{1,0:T(2,128)} %fb.1) | copy-start | bytes 388
  7.2 29.7 %all-gather.3.cloned.1.call-start = ((), (), s32[]{:S(2)}) async-start(), calls=%async_computation.5 | async-start | bytes 2621440 | tf_op jit(solution)/shard_map/all_gather | solution.py:103
  11.5 102.8 %reduce-scatter.2.cloned.1.call-start = ((), (), s32[]{:S(2)}) async-start(), calls=%async_computation.3 | async-start | bytes 2359296 | tf_op jit(solution)/shard_map/reduce_scatter | solution.py:122
  36.9 1.6 copy-start
  45.7 84.1 %copy-start.3 = (s32[2,4]{1,0:T(2,128)S(1)}, s32[2,4]{1,0:T(2,128)}, u32[]{:S(2)}) copy-start(s32[2,4]{1,0:T(2,128)} %param.9) | copy-start | bytes 100
  115.9 151.9 %copy-start.2 = (f32[2,256,256]{2,1,0:T(8,128)S(1)}, f32[2,256,256]{2,1,0:T(8,128)}, u32[]{:S(2)}) copy-start(f32[2,256,256]{2,1,0:T(8,128)} %param.8) | copy-start | bytes 1572868
  115.9 9.5 %all-to-all-start = ((f32[4,2,32,256]{3,2,1,0:T(8,128)}), f32[4,2,32,256]{3,2,1,0:T(8,128)S(1)}, u32[]{:S(2)}, u32[]{:S(2)}) async-start(f32[4,2,32,256]{3,2,1,0:T(8,128)} %copy.15), calls=%async_computation.1 | async-start | bytes 524288 | tf_op jit(solution)/shard_map/all_to_all | solution.py:133
  126.3 12.3 %all-to-all-start.1 = ((f32[4,2,32,256]{3,2,1,0:T(8,128)}), f32[4,2,32,256]{3,2,1,0:T(8,128)S(1)}, u32[]{:S(2)}, u32[]{:S(2)}) async-start(f32[4,2,32,256]{3,2,1,0:T(8,128)} %select_reduce_fusion.1), calls=%async_computation.2 | async-start | bytes 524288 | tf_op jit(solution)/shard_map/all_to_all | solution.py:140
  129.7 138.1 %all-reduce.2.cloned.1.call-start = ((), (), s32[]{:S(2)}) async-start(), calls=%async_computation.4 | async-start | bytes 1048576 | tf_op jit(solution)/shard_map/psum | solution.py:148
Sparse Core Ops, SparseCore 0:
  11.6 25.2 all-gather.2
  45.8 68.4 reduce-scatter.1
  141.1 126.6 all-reduce.1

commit v2 on v1

--- a/solution.py
+++ b/solution.py
@@ -74,7 +74,280 @@
             for s in range(nx):
                 for z in range(nz):
                     at = i * BS + (s * nz + z) * sub
-                    out[z * nx + s, f, i] = total[at : at + sub]
+                    out[f, s, i, z] = total[at : at + sub]
+
+
+MESH = pl.DeviceIdType.MESH
+
+
+def greet(peers):
+    barrier = pltpu.get_barrier_semaphore()
+    for peer in peers:
+        pl.semaphore_signal(barrier, inc=1, device_id=peer, device_id_type=MESH)
+    pl.semaphore_wait(barrier, len(peers))
+
+
+class Mail:
+    def __init__(self, send_sem, recv_sem):
+        self.send_sem, self.recv_sem = send_sem, recv_sem
+        self.sent = []
+
+    def send(self, src, dst, peer):
+        at = len(self.sent)
+        copy = pltpu.make_async_remote_copy(
+            src_ref=src,
+            dst_ref=dst,
+            send_sem=self.send_sem.at[at],
+            recv_sem=self.recv_sem.at[at],
+            device_id=peer,
+            device_id_type=MESH,
+        )
+        copy.start()
+        self.sent.append(copy)
+        return copy
+
+    def close(self):
+        for copy in self.sent:
+            copy.wait_send()
+
+
+def gather_kernel(dims, fb, panels, out, send_sem, recv_sem):
+    fronts, n_row, cg, cuts = dims
+    r = lax.axis_index("row")
+    c = lax.axis_index("col")
+    core, y, ny = lax.rem(r, 2), r // 2, n_row // 2
+    partner = r + 1 - 2 * core
+    lines = [lax.rem(y + d, ny) * 2 + core for d in range(1, ny)]
+    greet([(partner, c)] + [(line, c) for line in lines])
+    per_owner = panels.shape[1]
+    mail = Mail(send_sem, recv_sem)
+    height = BS // cuts
+    arriving, relayed = [], []
+    for f in range(fronts):
+        at = jnp.int32(0)
+        found = jnp.int32(0)
+        for j in range(per_owner):
+            hit = (fb[f, r * per_owner + j] // cg) == c
+            at = jnp.where(hit, j, at)
+            found = jnp.where(hit, 1, found)
+        out[r, f] = jnp.where(found == 1, panels[f, at], 0.0)
+        for h in range(cuts):
+            rows = pl.ds(h * height, height)
+            for d, line in enumerate(lines, 1):
+                piece = out.at[r, f, rows]
+                came = lax.rem(y + ny - d, ny) * 2 + core
+                arriving.append((mail.send(piece, piece, (line, c)), came, f, rows))
+        mine = out.at[r, f]
+        relayed.append(mail.send(mine, mine, (partner, c)))
+    for copy, came, f, rows in arriving:
+        copy.wait_recv()
+        piece = out.at[came, f, rows]
+        relayed.append(mail.send(piece, piece, (partner, c)))
+    for copy in relayed:
+        copy.wait_recv()
+    mail.close()
+
+
+def copies_of(dims):
+    fronts, kb, nr, nc, rg, cg, nz, nx = dims
+    n_row, n_col = kb // nr, kb // nc
+    total = nr * (nx - 1) + nr * (nz - 1) + (n_row - 1) + (nz - 1)
+    return fronts * (total + 2 * (1 + n_row // 2 - 1 + n_col - 1))
+
+
+def sum_kernel(dims, fb, partial, w, border, acc, xbuf, xs, zbuf, zs, slots, rbuf, qs, cbuf, ybuf, lbuf, red, send_sem, recv_sem):
+    fronts, kb, nr, nc, rg, cg, nz, nx = dims
+    n_row, n_col = kb // nr, kb // nc
+    per_owner = kb // n_row
+    r = lax.axis_index("row")
+    c = lax.axis_index("col")
+    s, z = lax.rem(c, nx), c // nx
+    core, y, ny = lax.rem(r, 2), r // 2, n_row // 2
+    partner = r + 1 - 2 * core
+    other = 1 - core
+    cols = [lax.rem(c + d, n_col) for d in range(1, n_col)]
+    rows = [lax.rem(r + d, n_row) for d in range(1, n_row)]
+    greet([(r, col) for col in cols] + [(row, c) for row in rows])
+    mail = Mail(send_sem, recv_sem)
+    width = w.shape[2]
+    share = w.shape[1]
+    part = acc.shape[4]
+    sub = zs.shape[2]
+
+    along_x = {}
+    for f in range(fronts):
+        for n in range(nr):
+            for d in range(1, nx):
+                to = lax.rem(s + d, nx)
+                along_x[f, n, d] = mail.send(
+                    partial.at[f, to, n], xbuf.at[f, n, d - 1], (r, z * nx + to)
+                )
+
+    along_z = {}
+
+    def x_sum(f, n):
+        for d in range(1, nx):
+            along_x[f, n, d].wait_recv()
+        total = partial[f, s, n]
+        for d in range(1, nx):
+            total = total + xbuf[f, n, d - 1]
+        xs[f, n] = total
+        for d in range(1, nz):
+            to = lax.rem(z + d, nz)
+            along_z[f, n, d] = mail.send(
+                xs.at[f, n, to], zbuf.at[f, n, d - 1], (r, to * nx + s)
+            )
+
+    def z_sum(f, n):
+        for d in range(1, nz):
+            along_z[f, n, d].wait_recv()
+        total = xs[f, n, z]
+        for d in range(1, nz):
+            total = total + zbuf[f, n, d - 1]
+        zs[f, n] = total
+
+    along_row = {}
+
+    def row_send(f):
+        if nr == n_row:
+            source = zs
+        else:
+            source = slots
+            n = jnp.int32(0)
+            for row in range(n_row):
+                named = jnp.int32(0)
+                for j in range(per_owner):
+                    named = jnp.where((fb[f, row * per_owner + j] // rg) == r, 1, named)
+                slots[f, row] = jnp.where(named == 1, zs[f, jnp.minimum(n, nr - 1)], 0.0)
+                n = n + named
+        rbuf[f][r] = source[f, r]
+        for d in range(1, n_row):
+            to = rows[d - 1]
+            along_row[f, d] = mail.send(source.at[f, to], rbuf[f].at[r], (to, c))
+
+    along_owner = {}
+
+    def owner_send(f):
+        for d in range(1, n_row):
+            along_row[f, d].wait_recv()
+        for q in range(nz):
+            qs[f, q] = rbuf[f][fb[f, r * per_owner + q] // rg]
+        border[f, z] = qs[f, z]
+        for d in range(1, nz):
+            to = lax.rem(z + d, nz)
+            along_owner[f, d] = mail.send(qs.at[f, to], border.at[f, z], (r, to * nx + s))
+
+    to_core = {}
+
+    def product(f):
+        for d in range(1, nz):
+            along_owner[f, d].wait_recv()
+        wh, wl = split(w[f])
+        ph, plo = split(jnp.concatenate([border[f, q] for q in range(nz)], axis=0))
+        dot = functools.partial(
+            lax.dot_general,
+            dimension_numbers=(((0,), (0,)), ((), ())),
+            preferred_element_type=jnp.float32,
+        )
+        total = dot(wh, ph) + (dot(wh, plo) + dot(wl, ph))
+        for a in range(2):
+            for b in range(ny):
+                for e in range(n_col):
+                    at = ((a * ny + b) * n_col + e) * part
+                    red[f, a, b, e] = total[at : at + part]
+        to_core[f] = mail.send(red.at[f, other], cbuf.at[f], (partner, c))
+
+    to_y = {}
+
+    def core_sum(f):
+        to_core[f].wait_recv()
+        red[f, core] = red[f, core] + cbuf[f]
+        for d in range(1, ny):
+            to = lax.rem(y + d, ny)
+            to_y[f, d] = mail.send(
+                red.at[f, core, to], ybuf.at[f, d - 1], (to * 2 + core, c)
+            )
+
+    to_col = {}
+
+    def y_sum(f):
+        for d in range(1, ny):
+            to_y[f, d].wait_recv()
+        total = red[f, core, y]
+        for d in range(1, ny):
+            total = total + ybuf[f, d - 1]
+        red[f, core, y] = total
+        for d in range(1, n_col):
+            to = cols[d - 1]
+            to_col[f, d] = mail.send(red.at[f, core, y, to], lbuf.at[f, d - 1], (r, to))
+
+    back_col = {}
+
+    def col_sum(f):
+        for d in range(1, n_col):
+            to_col[f, d].wait_recv()
+        total = red[f, core, y, c]
+        for d in range(1, n_col):
+            total = total + lbuf[f, d - 1]
+        acc[f, core, y, c] = total
+        mine = acc.at[f, core, y, c]
+        for d in range(1, n_col):
+            back_col[f, d] = mail.send(mine, mine, (r, cols[d - 1]))
+
+    back_y = {}
+
+    def y_back(f):
+        for d in range(1, n_col):
+            back_col[f, d].wait_recv()
+        mine = acc.at[f, core, y]
+        for d in range(1, ny):
+            to = lax.rem(y + d, ny)
+            back_y[f, d] = mail.send(mine, mine, (to * 2 + core, c))
+
+    back_core = {}
+
+    def core_back(f):
+        for d in range(1, ny):
+            back_y[f, d].wait_recv()
+        mine = acc.at[f, core]
+        back_core[f] = mail.send(mine, mine, (partner, c))
+
+    def finish(f):
+        back_core[f].wait_recv()
+
+    for n in range(nr):
+        x_sum(0, n)
+    for f in range(fronts):
+        for n in range(nr):
+            if f + 1 < fronts:
+                x_sum(f + 1, n)
+            z_sum(f, n)
+            if f > 0 and n == nr // 2 - 1:
+                owner_send(f - 1)
+        row_send(f)
+        if f > 0:
+            product(f - 1)
+    last = fronts - 1
+    owner_send(last)
+    for f in range(last):
+        core_sum(f)
+    product(last)
+    for f in range(last):
+        y_sum(f)
+    core_sum(last)
+    for f in range(last):
+        col_sum(f)
+    y_sum(last)
+    for f in range(last):
+        y_back(f)
+    col_sum(last)
+    for f in range(last):
+        core_back(f)
+    y_back(last)
+    core_back(last)
+    for f in range(fronts):
+        finish(f)
+    mail.close()
 
 
 def body(inverse, front_blocks, panels, diag_terms, bounds):
@@ -95,17 +368,26 @@
     sub = BS // n_col
     share = nz * sub
 
-    owner_rows = front_blocks.reshape(fronts, n_row, per_owner)
-    mine = lax.dynamic_index_in_dim(owner_rows, r, 1, keepdims=False)
-    pick = (mine // cg) == c
-    pieces = panels.reshape(fronts, per_owner, BS, width)
-    own_piece = jnp.sum(jnp.where(pick[:, :, None, None], pieces, 0.0), axis=1)
-    gathered = lax.all_gather(own_piece, "row", axis=0, tiled=False)
+    cuts = 2
+    gdims = (fronts, n_row, cg, cuts)
+    count = fronts * (cuts * 2 * (n_row // 2 - 1) + 1)
+    vmem = pl.BlockSpec(memory_space=pltpu.VMEM)
+    smem = pl.BlockSpec(memory_space=pltpu.SMEM)
+    gathered = pl.pallas_call(
+        functools.partial(gather_kernel, gdims),
+        out_shape=jax.ShapeDtypeStruct((n_row, fronts, BS, width), jnp.float32),
+        in_specs=[smem, vmem],
+        out_specs=vmem,
+        scratch_shapes=[pltpu.SemaphoreType.DMA((count,))] * 2,
+        compiler_params=pltpu.CompilerParams(
+            collective_id=0, has_side_effects=True, vmem_limit_bytes=24 << 20
+        ),
+    )(front_blocks, panels.reshape(fronts, per_owner, BS, width))
 
     dims = (fronts, kb, nr, nc, rg, cg, nz, nx)
     partial = pl.pallas_call(
         functools.partial(tile_kernel, dims),
-        out_shape=jax.ShapeDtypeStruct((n_col, fronts, nr, sub, width), jnp.float32),
+        out_shape=jax.ShapeDtypeStruct((fronts, nx, nr, nz, sub, width), jnp.float32),
         in_specs=[
             pl.BlockSpec(memory_space=pltpu.SMEM),
             pl.BlockSpec(memory_space=pl.ANY),
@@ -119,33 +401,40 @@
         compiler_params=pltpu.CompilerParams(vmem_limit_bytes=40 << 20),
     )(front_blocks, inverse, gathered)
 
-    reduced = lax.psum_scatter(partial, "col", scatter_dimension=0, tiled=False)
-    groups = front_blocks // rg
-    if nr == n_row:
-        slots = jnp.swapaxes(reduced, 0, 1)
-    else:
-        named = jnp.any((groups == r).reshape(fronts, n_row, per_owner), axis=-1)
-        place = jnp.cumsum(named.astype(jnp.int32), axis=1) - 1
-        chosen = named[:, :, None] & (place[:, :, None] == jnp.arange(nr))
-        slots = jnp.sum(
-            jnp.where(chosen.transpose(1, 0, 2)[..., None, None], reduced[None], 0.0), axis=2
-        )
-    received = lax.all_to_all(slots, "row", split_axis=0, concat_axis=0, tiled=True)
-    sources = lax.dynamic_index_in_dim(
-        groups.reshape(fronts, n_row, per_owner), r, 1, keepdims=False
-    )
-    chosen = sources.T[:, None, :] == jnp.arange(n_row, dtype=jnp.int32)[None, :, None]
-    ordered = jnp.sum(jnp.where(chosen[..., None, None], received[None], 0.0), axis=1)
-    lines = [[z * nx + s for z in range(nz)] for s in range(nx)]
-    product = lax.all_to_all(
-        ordered, "col", split_axis=0, concat_axis=0, axis_index_groups=lines, tiled=True
-    )
-    product = jnp.swapaxes(product, 0, 1).reshape(fronts, share, width)
     w_mine = lax.dynamic_slice_in_dim(panels, c * share, share, 1)
-    own_term = jnp.einsum(
-        "fsa,fsb->fab", w_mine, product, precision=lax.Precision.HIGHEST
-    )
-    summed = lax.psum(own_term, ("row", "col"))
+    ny = n_row // 2
+    part = width // (n_row * n_col)
+    count = copies_of(dims)
+    f32 = jnp.float32
+    border, acc = pl.pallas_call(
+        functools.partial(sum_kernel, dims),
+        out_shape=(
+            jax.ShapeDtypeStruct((fronts, nz, sub, width), f32),
+            jax.ShapeDtypeStruct((fronts, 2, ny, n_col, part, width), f32),
+        ),
+        in_specs=[smem, vmem, vmem],
+        out_specs=(vmem, vmem),
+        scratch_shapes=[
+            pltpu.VMEM((fronts, nr, nx - 1, nz, sub, width), f32),
+            pltpu.VMEM((fronts, nr, nz, sub, width), f32),
+            pltpu.VMEM((fronts, nr, nz - 1, sub, width), f32),
+            pltpu.VMEM((fronts, nr, sub, width), f32),
+            pltpu.VMEM((fronts, n_row, sub, width), f32),
+            [pltpu.VMEM((n_row, sub, width), f32)] * fronts,
+            pltpu.VMEM((fronts, nz, sub, width), f32),
+            pltpu.VMEM((fronts, ny, n_col, part, width), f32),
+            pltpu.VMEM((fronts, ny - 1, n_col, part, width), f32),
+            pltpu.VMEM((fronts, n_col - 1, part, width), f32),
+            pltpu.VMEM((fronts, 2, ny, n_col, part, width), f32),
+            pltpu.SemaphoreType.DMA((count,)),
+            pltpu.SemaphoreType.DMA((count,)),
+        ],
+        compiler_params=pltpu.CompilerParams(
+            collective_id=1, has_side_effects=True, vmem_limit_bytes=40 << 20
+        ),
+    )(front_blocks, partial, w_mine)
+    product = border.reshape(fronts, share, width)
+    summed = acc.reshape(fronts, width, width)
     ends = jnp.cumsum(bounds, axis=1)
     columns = jnp.arange(width, dtype=jnp.int32)
     ids = jnp.sum((columns[None, :, None] >= ends[:, None, :]).astype(jnp.int32), axis=2)

time: 277 us -> 90.9 us (0.33)
  waiting for transfers between devices: 234 us -> 0 us
  Pallas kernels: 7.14 us -> 84.7 us
  between operations: 13.8 us -> 0.7 us
  starting transfers between devices: 7.07 us -> 0 us
  other arithmetic: 7.18 us -> 1.93 us
    psum x1 -> x0, waiting for transfers between devices: 126 us -> none  [body(): summed = lax.psum(own_term, ('row', 'col'))]
    pallas_call x0 -> x2, Pallas kernels: none -> 78.9 us  [the longest x1 61.6 us: body(): pl.pallas_call(functools.partial(sum_kernel, dims), out_shape=(jax.ShapeD...]
    reduce_scatter x1 -> x0, waiting for transfers between devices: 68.5 us -> none  [body(): reduced = lax.psum_scatter(partial, 'col', scatter_dimension=0, tiled=False)]
    all_gather x1 -> x0, waiting for transfers between devices: 25.4 us -> none  [body(): gathered = lax.all_gather(own_piece, 'row', axis=0, tiled=False)]
    all_to_all x2 -> x0, waiting for transfers between devices: 14.6 us -> none  [the longest x1 8.62 us: body(): lax.all_to_all(ordered, 'col', split_axis=0, concat_axis=0, axis_index_gr...]
    all_to_all x2 -> x0, starting transfers between devices: 6.95 us -> none  [the longest x1 3.54 us: body(): lax.all_to_all(slots, 'row', split_axis=0, concat_axis=0, tiled=True)]
    reduce_sum x2 -> x0, other arithmetic: 3.5 us -> none  [the longest x1 2.66 us: body(): own_piece = jnp.sum(jnp.where(pick[:, :, None, None], pieces, 0.0), axis=1)]
  transfers between devices with their start and end apart: 5 -> 0, of which waited for: 5 -> 0; matrix products, arithmetic and copies ran while one was open for 0% -> 0% of each run, Pallas kernels for 0% -> 0%
where the time goes in v2:
time: 90.9 us; the launch traced here: 90.7 us
  Pallas kernels  84.7 us (93%)
  local copies, waits for them, and re-layouts  3.31 us (4%)
  other arithmetic  1.93 us (2%)
    pallas_call x1, Pallas kernels, body(): pl.pallas_call(functools.partial(sum_kernel, dims), out_shape=(jax.ShapeD...  61.6 us
    pallas_call x1, Pallas kernels, body(): pl.pallas_call(functools.partial(gather_kernel, gdims), out_shape=jax.Sha...  17.4 us
    pallas_call x1, Pallas kernels, body(): pl.pallas_call(functools.partial(tile_kernel, dims), out_shape=jax.ShapeD...  5.8 us
    unnamed x10, local copies, waits for them, and re-layouts  2.28 us

profile of v2, /device:TPU:0, one launch (start us, length us, event | category | flops | bytes accessed | tf_op | source)
XLA Modules:
  0.0 90.7 jit_solution(671706383263313529)
XLA Ops:
  0.6 0.0 copy-start
  0.6 1.6 %copy-done = f32[2,1024,256]{2,1,0:T(8,128)S(1)} copy-done((f32[2,1024,256]{2,1,0:T(8,128)S(1)}, f32[2,1024,256]{2,1,0:T(8,128)}, u32[]{:S(2)}) %copy-start) | copy-done | bytes 2097176
  2.2 0.0 copy-start.1
  2.2 0.7 copy-done.1
  2.9 0.0 copy-start.2
  2.9 17.4 %shard_map.68.w = f32[4,2,256,256]{3,2,1,0:T(8,128)S(1)} custom-call(s32[2,16]{1,0:T(2,128)S(1)} %copy-done.1, f32[2,4,256,256]{3,2,1,0:T(8,128)S(1)} %bitcast.6), custom_call_target="tpu_custom_call" | custom-call | tf_op jit(solution)/shard_map/pallas_call | solution.py:376
  20.3 0.0 copy-done.2
  20.3 5.8 %shard_map.69.partial = f32[2,2,4,4,32,256]{5,4,3,2,1,0:T(8,128)S(1)} custom-call(s32[2,16]{1,0:T(2,128)S(1)} %copy-done.2, f32[4096,2048]{1,0:T(8,128)} %inv.1, f32[4,2,256,256]{3,2,1,0:T(8,128)S(1)} %shard_map.68.w), custom_call_target="tpu_custom_call" | custom-call | tf_op jit(solution)/shard_map/pallas_call | solution.py:388
  26.1 0.0 copy-start.4
  26.1 0.0 copy-start.3
  26.1 1.0 %constant_dynamic-slice_fusion.w = f32[2,128,256]{2,1,0:T(8,128)S(1)} fusion(f32[2,1024,256]{2,1,0:T(8,128)} %param.7, s32[]{:T(128)S(6)} %select_n.3), kind=kLoop, calls=%fused_computation.4 | loop fusion | bytes 524292 | tf_op jit(solution)/shard_map/dynamic_slice | solution.py:404
  27.2 61.6 %shard_map.70 = (f32[2,4,32,256]{3,2,1,0:T(8,128)S(1)}, f32[2,2,2,8,8,256]{5,4,3,2,1,0:T(8,128)S(1)}) custom-call(s32[2,16]{1,0:T(2,128)S(1)} %copy-done.2, f32[2,2,4,4,32,256]{5,4,3,2,1,0:T(8,128)S(1)} %shard_map.69.partial, f32[2,128,256]{2,1,0:T(8,128)S(1)} %constant_dynamic-slice_fusion.w), custom_call_target="tpu_custom_call" | custom-call | tf_op jit(solution)/shard_map/pallas_call | solution.py:409
  88.7 0.7 neg.6
  89.5 0.0 copy-done.4
  89.5 0.2 reduce_window_sum.11
  89.6 0.1 convert_reduce_fusion
  89.7 0.0 copy-done.3
  89.7 0.9 %fusion = f32[2,256,256]{2,1,0:T(8,128)} fusion(f32[2,256,256]{2,1,0:T(8,128)S(1)} %copy-done.3, f32[2,2,2,8,8,256]{5,4,3,2,1,0:T(8,128)S(1)} %get-tuple-element.5, s32[2,256]{1,0:T(2,128)S(1)} %convert_reduce_fusion), kind=kLoop, calls=%fused_computation.1 | loop fusion | flops 393216 | bytes 1574912 | tf_op jit(solution)/shard_map/mul | solution.py:442
Async XLA Ops:
  0.6 1.6 %copy-start = (f32[2,1024,256]{2,1,0:T(8,128)S(1)}, f32[2,1024,256]{2,1,0:T(8,128)}, u32[]{:S(2)}) copy-start(f32[2,1024,256]{2,1,0:T(8,128)} %param.7) | copy-start | bytes 6291460
  2.2 0.7 copy-start.1
  2.9 17.4 %copy-start.2 = (s32[2,16]{1,0:T(2,128)S(1)}, s32[2,16]{1,0:T(2,128)}, u32[]{:S(2)}) copy-start(s32[2,16]{1,0:T(2,128)} %fb.5) | copy-start | bytes 388
  26.1 63.4 %copy-start.4 = (s32[2,4]{1,0:T(2,128)S(1)}, s32[2,4]{1,0:T(2,128)}, u32[]{:S(2)}) copy-start(s32[2,4]{1,0:T(2,128)} %param.9) | copy-start | bytes 100
  26.1 63.6 %copy-start.3 = (f32[2,256,256]{2,1,0:T(8,128)S(1)}, f32[2,256,256]{2,1,0:T(8,128)}, u32[]{:S(2)}) copy-start(f32[2,256,256]{2,1,0:T(8,128)} %param.8) | copy-start | bytes 1572868

commit v3 on v2

--- a/solution.py
+++ b/solution.py
@@ -169,8 +169,7 @@
     rows = [lax.rem(r + d, n_row) for d in range(1, n_row)]
     greet([(r, col) for col in cols] + [(row, c) for row in rows])
     mail = Mail(send_sem, recv_sem)
-    width = w.shape[2]
-    share = w.shape[1]
+    share = border.shape[1] * border.shape[2]
     part = acc.shape[4]
     sub = zs.shape[2]
 
@@ -242,7 +241,7 @@
     def product(f):
         for d in range(1, nz):
             along_owner[f, d].wait_recv()
-        wh, wl = split(w[f])
+        wh, wl = split(w[f, pl.ds(pl.multiple_of(c * share, share), share)])
         ph, plo = split(jnp.concatenate([border[f, q] for q in range(nz)], axis=0))
         dot = functools.partial(
             lax.dot_general,
@@ -315,38 +314,25 @@
     def finish(f):
         back_core[f].wait_recv()
 
-    for n in range(nr):
-        x_sum(0, n)
+    tail = (row_send, owner_send, product, core_sum, y_sum, col_sum, y_back, core_back, finish)
+    steps = []
     for f in range(fronts):
-        for n in range(nr):
-            if f + 1 < fronts:
-                x_sum(f + 1, n)
-            z_sum(f, n)
-            if f > 0 and n == nr // 2 - 1:
-                owner_send(f - 1)
-        row_send(f)
-        if f > 0:
-            product(f - 1)
-    last = fronts - 1
-    owner_send(last)
-    for f in range(last):
-        core_sum(f)
-    product(last)
-    for f in range(last):
-        y_sum(f)
-    core_sum(last)
-    for f in range(last):
-        col_sum(f)
-    y_sum(last)
-    for f in range(last):
-        y_back(f)
-    col_sum(last)
-    for f in range(last):
-        core_back(f)
-    y_back(last)
-    core_back(last)
-    for f in range(fronts):
-        finish(f)
+        heads = [functools.partial(x_sum, f, n) for n in range(nr)]
+        mids = [functools.partial(z_sum, f, n) for n in range(nr)]
+        ends = [functools.partial(step, f) for step in tail]
+        steps.append(heads + mids + ends)
+    for step in steps[0][:nr]:
+        step()
+    ahead = steps[0][nr:]
+    for later in steps[1:]:
+        for i, step in enumerate(later):
+            step()
+            count = 2 if i < 2 or i == 3 else 1
+            for move in ahead[:count]:
+                move()
+            ahead = ahead[count:]
+    for move in ahead:
+        move()
     mail.close()
 
 
@@ -401,7 +387,6 @@
         compiler_params=pltpu.CompilerParams(vmem_limit_bytes=40 << 20),
     )(front_blocks, inverse, gathered)
 
-    w_mine = lax.dynamic_slice_in_dim(panels, c * share, share, 1)
     ny = n_row // 2
     part = width // (n_row * n_col)
     count = copies_of(dims)
@@ -432,7 +417,7 @@
         compiler_params=pltpu.CompilerParams(
             collective_id=1, has_side_effects=True, vmem_limit_bytes=40 << 20
         ),
-    )(front_blocks, partial, w_mine)
+    )(front_blocks, partial, panels)
     product = border.reshape(fronts, share, width)
     summed = acc.reshape(fronts, width, width)
     ends = jnp.cumsum(bounds, axis=1)

time: 90.9 us -> 104 us (1.14)
  Pallas kernels: 84.7 us -> 98.5 us
    pallas_call x1, Pallas kernels: 61.6 us -> 75.4 us  [body(): pl.pallas_call(functools.partial(sum_kernel, dims), out_shape=(jax.ShapeD...]
    unnamed x10 -> x12, local copies, waits for them, and re-layouts: 2.28 us -> 2.29 us
where the time goes in v3:
time: 104 us; the launch traced here: 103 us
  Pallas kernels  98.5 us (95%)
  local copies, waits for them, and re-layouts  2.29 us (2%)
  other arithmetic  1.92 us (2%)
    pallas_call x1, Pallas kernels, body(): pl.pallas_call(functools.partial(sum_kernel, dims), out_shape=(jax.ShapeD...  75.4 us
    pallas_call x1, Pallas kernels, body(): pl.pallas_call(functools.partial(gather_kernel, gdims), out_shape=jax.Sha...  17.4 us
    pallas_call x1, Pallas kernels, body(): pl.pallas_call(functools.partial(tile_kernel, dims), out_shape=jax.ShapeD...  5.8 us
    unnamed x12, local copies, waits for them, and re-layouts  2.29 us

profile of v3, /device:TPU:0, one launch (start us, length us, event | category | flops | bytes accessed | tf_op | source)
XLA Modules:
  0.0 103.5 jit_solution(11001153003378010703)
XLA Ops:
  0.6 0.0 copy-start
  0.6 1.6 %copy-done = f32[2,1024,256]{2,1,0:T(8,128)S(1)} copy-done((f32[2,1024,256]{2,1,0:T(8,128)S(1)}, f32[2,1024,256]{2,1,0:T(8,128)}, u32[]{:S(2)}) %copy-start) | copy-done | bytes 2097176
  2.2 0.0 copy-start.2
  2.2 0.7 copy-done.2
  2.9 0.0 copy-start.3
  2.9 17.4 %shard_map.68.w = f32[4,2,256,256]{3,2,1,0:T(8,128)S(1)} custom-call(s32[2,16]{1,0:T(2,128)S(1)} %copy-done.2, f32[2,4,256,256]{3,2,1,0:T(8,128)S(1)} %bitcast.6), custom_call_target="tpu_custom_call" | custom-call | tf_op jit(solution)/shard_map/pallas_call | solution.py:362
  20.3 0.0 copy-done.3
  20.3 0.0 copy-start.1
  20.3 5.8 %shard_map.69.partial = f32[2,2,4,4,32,256]{5,4,3,2,1,0:T(8,128)S(1)} custom-call(s32[2,16]{1,0:T(2,128)S(1)} %copy-done.3, f32[4096,2048]{1,0:T(8,128)} %inv.1, f32[4,2,256,256]{3,2,1,0:T(8,128)S(1)} %shard_map.68.w), custom_call_target="tpu_custom_call" | custom-call | tf_op jit(solution)/shard_map/pallas_call | solution.py:374
  26.1 0.0 copy-done.1
  26.1 0.0 copy-start.5
  26.1 0.0 copy-start.4
  26.1 75.4 %shard_map.70 = (f32[2,4,32,256]{3,2,1,0:T(8,128)S(1)}, f32[2,2,2,8,8,256]{5,4,3,2,1,0:T(8,128)S(1)}) custom-call(s32[2,16]{1,0:T(2,128)S(1)} %copy-done.3, f32[2,2,4,4,32,256]{5,4,3,2,1,0:T(8,128)S(1)} %shard_map.69.partial, f32[2,1024,256]{2,1,0:T(8,128)S(1)} %copy-done.1), custom_call_target="tpu_custom_call" | custom-call | tf_op jit(solution)/shard_map/pallas_call | solution.py:394
  101.5 0.0 copy-done.5
  101.5 0.2 reduce_window_sum.11
  101.7 0.1 convert_reduce_fusion
  101.8 0.0 copy-done.4
  101.8 0.9 fusion
  102.7 0.7 neg.6
Async XLA Ops:
  0.6 1.6 %copy-start = (f32[2,1024,256]{2,1,0:T(8,128)S(1)}, f32[2,1024,256]{2,1,0:T(8,128)}, u32[]{:S(2)}) copy-start(f32[2,1024,256]{2,1,0:T(8,128)} %w.1) | copy-start | bytes 6291460
  2.2 0.7 copy-start.2
  2.9 17.4 %copy-start.3 = (s32[2,16]{1,0:T(2,128)S(1)}, s32[2,16]{1,0:T(2,128)}, u32[]{:S(2)}) copy-start(s32[2,16]{1,0:T(2,128)} %fb.5) | copy-start | bytes 388
  20.3 5.8 %copy-start.1 = (f32[2,1024,256]{2,1,0:T(8,128)S(1)}, f32[2,1024,256]{2,1,0:T(8,128)}, u32[]{:S(2)}) copy-start(f32[2,1024,256]{2,1,0:T(8,128)} %w.1) | copy-start | bytes 6291460
  26.1 75.4 %copy-start.5 = (s32[2,4]{1,0:T(2,128)S(1)}, s32[2,4]{1,0:T(2,128)}, u32[]{:S(2)}) copy-start(s32[2,4]{1,0:T(2,128)} %param.9) | copy-start | bytes 100
  26.1 75.7 %copy-start.4 = (f32[2,256,256]{2,1,0:T(8,128)S(1)}, f32[2,256,256]{2,1,0:T(8,128)}, u32[]{:S(2)}) copy-start(f32[2,256,256]{2,1,0:T(8,128)} %param.8) | copy-start | bytes 1572868
